TPU v7x, 32 devices: a whole 2x2x4 slice. The times are simulated.
32 devices in a mesh: batch: 4 (over x, core), neuron: 8 (over z, y).
Axes of the slice: x: 2, y: 2, z: 4, core: 2. Of those that a mesh axis runs over, the one named last changes fastest.
Arguments:
- tokens: bfloat16 [2, 256, 12288], P(None, 'neuron', 'batch'), may hold values from -6 to 6
- ln_gain: float32 [12288], P('batch'), may hold values from 0.25 to 1.75
- ln_bias: float32 [12288], P('batch'), may hold values from -3 to 3
- up_weight: bfloat16 [12288, 24576], P('batch', 'neuron'), may hold values from -0.0546875 to 0.0546875
- up_bias: float32 [24576], P('neuron'), may hold values from -3 to 3
- down_weight: bfloat16 [24576, 12288], P('neuron', 'batch'), may hold values from -0.078125 to 0.078125
- down_bias: float32 [12288], P('batch'), may hold values from -3 to 3
- active: int32 [2, 2, 48], replicated, may hold values from 0 to 191, all different within a row
Outputs:
- mixed: bfloat16 [2, 256, 12288], P(None, 'neuron', 'batch')
Inputs may be any that keep to these rules, and one draw needn't show every extreme that they name: `active`: each row block of each; despite its name it splits features, not a batch step lists 48 distinct neuron block numbers; every number appears in some list.
All inputs are finite; a program needn't handle non-finite values.
Results may differ from a plain program's by a relative error of at most 0.0044.
Values may be sent and summed in bfloat16 or wider, within the bound.
No kernel may reach another device: no remote copies, remote signals or barrier semaphores. Data moves between devices by JAX's collectives and lax.ppermute only.
A program may use at most 128 MiB of HBM per device.

v0:
```python
import jax
import jax.numpy as jnp
from jax import lax
from jax.sharding import PartitionSpec as P

D = 12288
BLK = 128
RB = 128
STEPS = 2
epsilon = 1e-05


def local_table(listed, first_block, local_blocks):
    block_ids = first_block + jnp.arange(local_blocks, dtype=jnp.int32)
    return jnp.any(listed[:, :, None] == block_ids[None, None, :], axis=1).astype(jnp.float32)


def activate(preact, up_bias, table, first_row):
    row_total = preact.shape[0]
    local_blocks = table.shape[1]
    row_blocks = (first_row + jnp.arange(row_total, dtype=jnp.int32)) // RB
    block_count = table.shape[0]
    onehot = (row_blocks[:, None] == jnp.arange(block_count, dtype=jnp.int32)[None, :]).astype(
        jnp.float32
    )
    row_mask = jnp.dot(onehot, table, preferred_element_type=jnp.float32)
    shaped = jnp.maximum(preact + up_bias, 0.0).reshape(row_total, local_blocks, BLK)
    return (
        (shaped * row_mask[:, :, None]).reshape(row_total, local_blocks * BLK).astype(jnp.bfloat16)
    )


def normalize(inputs, sum_total, square_total, ln_gain, ln_bias):
    average = sum_total / D
    spread = square_total / D - average * average
    scaled = (inputs - average[:, None]) * lax.rsqrt(spread + epsilon)[:, None]
    return (scaled * ln_gain + ln_bias).astype(jnp.bfloat16)


def local(tokens, ln_gain, ln_bias, up_weight, up_bias, down_weight, down_bias, active):
    local_rows = tokens.shape[1]
    local_neurons = up_weight.shape[1]
    local_blocks = local_neurons // BLK
    neuron_index = lax.axis_index("neuron")
    batch_index = lax.axis_index("batch")
    all_rows = local_rows * lax.axis_size("neuron")
    share_rows = all_rows // lax.axis_size("batch")
    first_block = neuron_index * local_blocks
    results = []
    for step_index in range(STEPS):
        residual = tokens[step_index]
        residual_wide = residual.astype(jnp.float32)
        table = local_table(active[step_index], first_block, local_blocks)
        sum_total, square_total = lax.psum(
            (jnp.sum(residual_wide, axis=-1), jnp.sum(residual_wide * residual_wide, axis=-1)),
            "batch",
        )
        normed = normalize(residual_wide, sum_total, square_total, ln_gain, ln_bias)
        gathered = lax.all_gather(normed, "neuron", axis=0, tiled=True)
        preact = lax.psum_scatter(
            jnp.dot(gathered, up_weight, preferred_element_type=jnp.float32),
            "batch",
            scatter_dimension=0,
            tiled=True,
        )
        hidden_share = activate(preact, up_bias, table, batch_index * share_rows)
        hidden_all = lax.all_gather(hidden_share, "batch", axis=0, tiled=True)
        projected = lax.psum_scatter(
            jnp.dot(hidden_all, down_weight, preferred_element_type=jnp.float32),
            "neuron",
            scatter_dimension=0,
            tiled=True,
        )
        results.append((projected + residual_wide + down_bias).astype(jnp.bfloat16))
    return jnp.stack(results)


def solution(mesh):
    in_specs = (
        P(None, "neuron", "batch"),
        P("batch"),
        P("batch"),
        P("batch", "neuron"),
        P("neuron"),
        P("neuron", "batch"),
        P("batch"),
        P(),
    )
    out_specs = P(None, "neuron", "batch")
    return jax.shard_map(local, mesh=mesh, in_specs=in_specs, out_specs=out_specs, check_vma=False)
```

profile of v0, /device:TPU:0, one launch (start us, length us, event | category | flops | bytes accessed | tf_op | source)
XLA Modules:
  0.0 396.0 jit_solution(5214317015410200735)
XLA Ops:
  6.5 0.0 all-gather.5.cloned.1.call-start
  6.5 1.2 convert_reduce_fusion.1
  7.7 1.2 fusion.12
  8.9 8.4 %all-reduce = (f32[32]{0:T(128)S(1)}, f32[32]{0:T(128)S(1)}, f32[32]{0:T(128)S(1)}, f32[32]{0:T(128)S(1)}) all-reduce(f32[32]{0:T(128)S(1)} %get-tuple-element.8, f32[32]{0:T(128)S(1)} %get-tuple-element.6, f32[32]{0:T(128)S(1)} %get-tuple-element.7, f32[32]{0:T(128)S(1)} %get-tuple-element.5), channel_id=1, replica_groups=mesh['batch'=4,'neuron'=8] {'batch'}, use_global_device_ids=true, to_apply=%region_10.11 | all-reduce | flops 128 | bytes 1024 | tf_op jit(solution)/shard_map/psum | solution.py:54
  17.3 2.0 fusion.11
  19.3 0.0 all-gather.5.cloned.1.call-update
  19.3 0.0 all-gather.9.cloned.1.call-start
  19.4 0.7 all-gather.9.cloned.1.call-update
  20.1 0.0 reduce-scatter.5.cloned.1.call-start
  20.1 43.9 %all-gather.5.cloned.1.call-done = bf16[256,3072]{1,0:T(8,128)(2,1)} async-done(((bf16[32,3072]{1,0:T(8,128)(2,1)}), bf16[256,3072]{1,0:T(8,128)(2,1)}) %all-gather.5.cloned.1.call-update) | async-done | bytes 1572880 | tf_op jit(solution)/shard_map/all_gather | solution.py:59
  64.0 10.6 %fusion.28 = f32[256,3072]{1,0:T(8,128)} fusion(bf16[256,3072]{1,0:T(8,128)(2,1)} %all-gather.5.cloned.1.call-done, bf16[3072,3072]{1,0:T(8,128)(2,1)} %param.11), kind=kOutput, calls=%fused_computation.49 | convolution fusion | flops 4831838208 | bytes 23592960 | tf_op jit(solution)/shard_map/dot_general | solution.py:61
  74.6 0.0 reduce-scatter.5.cloned.1.call-update
  74.6 0.0 reduce-scatter.9.cloned.1.call-start
  74.6 34.2 %all-gather.9.cloned.1.call-done = bf16[256,3072]{1,0:T(8,128)(2,1)} async-done(((bf16[32,3072]{1,0:T(8,128)(2,1)}), bf16[256,3072]{1,0:T(8,128)(2,1)}) %all-gather.9.cloned.1.call-update) | async-done | bytes 1572880 | tf_op jit(solution)/shard_map/all_gather | solution.py:59
  108.8 11.1 %fusion.30 = f32[256,3072]{1,0:T(8,128)} fusion(bf16[256,3072]{1,0:T(8,128)(2,1)} %all-gather.9.cloned.1.call-done, bf16[3072,3072]{1,0:T(8,128)(2,1)} %param.11), kind=kOutput, calls=%fused_computation.51 | convolution fusion | flops 4831838208 | bytes 23592960 | tf_op jit(solution)/shard_map/dot_general | solution.py:61
  119.9 0.0 copy-start.3
  119.9 0.0 copy-start.1
  119.9 0.0 reduce-scatter.9.cloned.1.call-update
  119.9 0.0 all-gather.11.cloned.1.call-start
  120.0 0.6 copy-done.3
  120.6 0.2 compare_reduce_fusion.1
  120.8 0.2 fusion.24
  121.0 0.2 fusion.25
  121.2 26.4 %reduce-scatter.5.cloned.1.call-done = f32[64,3072]{1,0:T(8,128)} async-done(((f32[256,3072]{1,0:T(8,128)}), f32[64,3072]{1,0:T(8,128)}) %reduce-scatter.5.cloned.1.call-update) | async-done | bytes 786448 | tf_op jit(solution)/shard_map/reduce_scatter | solution.py:60
  147.6 40.3 %reduce-scatter.9.cloned.1.call-done = f32[64,3072]{1,0:T(8,128)} async-done(((f32[256,3072]{1,0:T(8,128)}), f32[64,3072]{1,0:T(8,128)}) %reduce-scatter.9.cloned.1.call-update) | async-done | bytes 786448 | tf_op jit(solution)/shard_map/reduce_scatter | solution.py:60
  187.9 0.3 mul.87
  188.2 0.3 mul.79
  188.5 0.0 copy-done.1
  188.5 2.7 fusion.1
  191.2 0.0 all-gather.11.cloned.1.call-update
  191.2 0.0 all-gather.7.cloned.1.call-start
  191.2 0.5 all-gather.7.cloned.1.call-update
  191.8 0.0 reduce-scatter.11.cloned.1.call-start
  191.8 19.2 %all-gather.11.cloned.1.call-done = bf16[256,3072]{1,0:T(8,128)(2,1)} async-done(((bf16[64,3072]{1,0:T(8,128)(2,1)}), bf16[256,3072]{1,0:T(8,128)(2,1)}) %all-gather.11.cloned.1.call-update) | async-done | bytes 1572880 | tf_op jit(solution)/shard_map/all_gather | solution.py:67
  211.0 10.6 %fusion.31 = f32[256,3072]{1,0:T(8,128)} fusion(bf16[256,3072]{1,0:T(8,128)(2,1)} %all-gather.11.cloned.1.call-done, bf16[3072,3072]{1,0:T(8,128)(2,1)} %param.13), kind=kOutput, calls=%fused_computation.52 | convolution fusion | flops 4831838208 | bytes 23592960 | tf_op jit(solution)/shard_map/dot_general | solution.py:69
  221.5 0.0 reduce-scatter.11.cloned.1.call-update
  221.6 0.0 reduce-scatter.7.cloned.1.call-start
  221.6 10.4 %all-gather.7.cloned.1.call-done = bf16[256,3072]{1,0:T(8,128)(2,1)} async-done(((bf16[64,3072]{1,0:T(8,128)(2,1)}), bf16[256,3072]{1,0:T(8,128)(2,1)}) %all-gather.7.cloned.1.call-update) | async-done | bytes 1572880 | tf_op jit(solution)/shard_map/all_gather | solution.py:67
  232.1 10.6 %fusion.29 = f32[256,3072]{1,0:T(8,128)} fusion(bf16[256,3072]{1,0:T(8,128)(2,1)} %all-gather.7.cloned.1.call-done, bf16[3072,3072]{1,0:T(8,128)(2,1)} %param.13), kind=kOutput, calls=%fused_computation.50 | convolution fusion | flops 4831838208 | bytes 23592960 | tf_op jit(solution)/shard_map/dot_general | solution.py:69
  242.6 0.0 copy-start
  242.6 0.0 reduce-scatter.7.cloned.1.call-update
  242.7 67.5 %reduce-scatter.11.cloned.1.call-done = f32[32,3072]{1,0:T(8,128)} async-done(((f32[256,3072]{1,0:T(8,128)}), f32[32,3072]{1,0:T(8,128)}) %reduce-scatter.11.cloned.1.call-update) | async-done | bytes 393232 | tf_op jit(solution)/shard_map/reduce_scatter | solution.py:68
  310.1 77.1 %reduce-scatter.7.cloned.1.call-done = f32[32,3072]{1,0:T(8,128)} async-done(((f32[256,3072]{1,0:T(8,128)}), f32[32,3072]{1,0:T(8,128)}) %reduce-scatter.7.cloned.1.call-update) | async-done | bytes 393232 | tf_op jit(solution)/shard_map/reduce_scatter | solution.py:68
  387.2 0.0 copy-done
  387.2 0.0 copy-done.2
  387.2 1.2 fusion.23
  388.4 0.0 copy-start.4
  388.4 0.7 copy-done.4
  (6 shorter events, 0.0 us)
Async XLA Ops:
  6.5 57.5 %all-gather.5.cloned.1.call-start = ((), (), s32[]{:S(2)}) async-start(), calls=%async_computation.4 | async-start | bytes 1769472 | tf_op jit(solution)/shard_map/all_gather | solution.py:59
  19.3 89.5 %all-gather.9.cloned.1.call-start = ((), (), s32[]{:S(2)}) async-start(), calls=%async_computation.8 | async-start | bytes 1769472 | tf_op jit(solution)/shard_map/all_gather | solution.py:59
  20.1 127.5 %reduce-scatter.5.cloned.1.call-start = ((), (), s32[]{:S(2)}) async-start(), calls=%async_computation.5 | async-start | bytes 3932160 | tf_op jit(solution)/shard_map/reduce_scatter | solution.py:60
  74.6 113.3 %reduce-scatter.9.cloned.1.call-start = ((), (), s32[]{:S(2)}) async-start(), calls=%async_computation.9 | async-start | bytes 3932160 | tf_op jit(solution)/shard_map/reduce_scatter | solution.py:60
  119.9 0.7 copy-start.3
  119.9 68.6 %copy-start.1 = (f32[3072]{0:T(1024)S(1)}, f32[3072]{0:T(1024)}, u32[]{:S(2)}) copy-start(f32[3072]{0:T(1024)} %param.12) | copy-start | bytes 36868
  119.9 91.1 %all-gather.11.cloned.1.call-start = ((), (), s32[]{:S(2)}) async-start(), calls=%async_computation.10 | async-start | bytes 1966080 | tf_op jit(solution)/shard_map/all_gather | solution.py:67
  191.2 40.9 %all-gather.7.cloned.1.call-start = ((), (), s32[]{:S(2)}) async-start(), calls=%async_computation.6 | async-start | bytes 1966080 | tf_op jit(solution)/shard_map/all_gather | solution.py:67
  191.8 118.4 %reduce-scatter.11.cloned.1.call-start = ((), (), s32[]{:S(2)}) async-start(), calls=%async_computation.11 | async-start | bytes 3538944 | tf_op jit(solution)/shard_map/reduce_scatter | solution.py:68
  221.6 165.6 %reduce-scatter.7.cloned.1.call-start = ((), (), s32[]{:S(2)}) async-start(), calls=%async_computation.7 | async-start | bytes 3538944 | tf_op jit(solution)/shard_map/reduce_scatter | solution.py:68
  242.6 144.6 %copy-start = (bf16[2,32,3072]{2,1,0:T(8,128)(2,1)S(1)}, bf16[2,32,3072]{2,1,0:T(8,128)(2,1)}, u32[]{:S(2)}) copy-start(bf16[2,32,3072]{2,1,0:T(8,128)(2,1)} %param.8) | copy-start | bytes 1179652
  242.6 144.6 %copy-start.2 = (f32[3072]{0:T(1024)S(1)}, f32[3072]{0:T(1024)}, u32[]{:S(2)}) copy-start(f32[3072]{0:T(1024)} %param.14) | copy-start | bytes 36868
  388.4 0.7 copy-start.4
Sparse Core Ops, SparseCore 0:
  19.5 44.4 all-gather.4
  66.2 42.5 all-gather.8
  111.4 36.2 reduce-scatter.4
  150.0 37.8 reduce-scatter.8
  191.3 19.6 all-gather.10
  212.4 19.6 all-gather.6
  235.6 74.4 reduce-scatter.10
  313.7 73.4 reduce-scatter.6
where the time goes:
time: 396 us
  waiting for transfers between devices  320 us (81%)
  matrix products  43.2 us (11%)
  between operations  13.6 us (3%)
  other arithmetic  8.54 us (2%)
  blocking collectives  8.37 us (2%)
    reduce_scatter x2, waiting for transfers between devices, local(): lax.psum_scatter(jnp.dot(hidden_all, down_weight, preferred_element_type=...  145 us
    all_gather x2, waiting for transfers between devices, local(): gathered = lax.all_gather(normed, 'neuron', axis=0, tiled=True)  78 us
    reduce_scatter x2, waiting for transfers between devices, local(): lax.psum_scatter(jnp.dot(gathered, up_weight, preferred_element_type=jnp....  66.7 us
    all_gather x2, waiting for transfers between devices, local(): hidden_all = lax.all_gather(hidden_share, 'batch', axis=0, tiled=True)  29.6 us
    dot_general x2, matrix products, local(): jnp.dot(gathered, up_weight, preferred_element_type=jnp.float32)  21.6 us
    dot_general x2, matrix products, local(): jnp.dot(hidden_all, down_weight, preferred_element_type=jnp.float32)  21.2 us
    psum x1, blocking collectives, local(): lax.psum((jnp.sum(residual_wide, axis=-1), jnp.sum(residual_wide * residu...  8.37 us
  transfers between devices with their start and end apart: 8, of which 8 were waited for; matrix products, arithmetic and copies ran while one was open for 11% of the time, Pallas kernels for 0%

commit v1 on v0

--- a/solution.py
+++ b/solution.py
@@ -56,7 +56,15 @@
             "batch",
         )
         normed = normalize(residual_wide, sum_total, square_total, ln_gain, ln_bias)
-        gathered = lax.all_gather(normed, "neuron", axis=0, tiled=True)
+        ways, here = (lax.axis_size("neuron"), lax.axis_index("neuron"))
+        grown, reach = (normed, 1)
+        while reach < ways:
+            theirs = lax.ppermute(grown, "neuron", [(d, d ^ reach) for d in range(ways)])
+            mine_first = jnp.concatenate([grown, theirs], axis=0)
+            theirs_first = jnp.concatenate([theirs, grown], axis=0)
+            grown = jnp.where(here & reach == 0, mine_first, theirs_first)
+            reach = 2 * reach
+        gathered = grown
         preact = lax.psum_scatter(
             jnp.dot(gathered, up_weight, preferred_element_type=jnp.float32),
             "batch",

time: 396 us -> 390 us (0.985)
  waiting for transfers between devices: 320 us -> 302 us
  starting transfers between devices: 0.29 us -> 13.9 us
    ppermute x0 -> x6, waiting for transfers between devices: none -> 87.2 us  [local(): lax.ppermute(grown, 'neuron', [(d, d ^ reach) for d in range(ways)])]
    all_gather x2 -> x0, waiting for transfers between devices: 78 us -> none  [local(): gathered = lax.all_gather(normed, 'neuron', axis=0, tiled=True)]
    reduce_scatter x2, waiting for transfers between devices: 66.7 us -> 40.4 us  [local(): lax.psum_scatter(jnp.dot(gathered, up_weight, preferred_element_type=jnp....]
    ppermute x0 -> x6, starting transfers between devices: none -> 13.7 us  [local(): lax.ppermute(grown, 'neuron', [(d, d ^ reach) for d in range(ways)])]
  transfers between devices with their start and end apart: 8 -> 12, of which waited for: 8 -> 11; matrix products, arithmetic and copies ran while one was open for 11% -> 8% of each run, Pallas kernels for 0% -> 0%
where the time goes in v1:
time: 390 us
  waiting for transfers between devices  302 us (77%)
  matrix products  43 us (11%)
  starting transfers between devices  13.9 us (4%)
  between operations  13.6 us (3%)
  blocking collectives  8.37 us (2%)
  other arithmetic  6.87 us (2%)
    reduce_scatter x2, waiting for transfers between devices, local(): lax.psum_scatter(jnp.dot(hidden_all, down_weight, preferred_element_type=...  144 us
    ppermute x6, waiting for transfers between devices, local(): lax.ppermute(grown, 'neuron', [(d, d ^ reach) for d in range(ways)])  87.2 us
    reduce_scatter x2, waiting for transfers between devices, local(): lax.psum_scatter(jnp.dot(gathered, up_weight, preferred_element_type=jnp....  40.4 us
    all_gather x2, waiting for transfers between devices, local(): hidden_all = lax.all_gather(hidden_share, 'batch', axis=0, tiled=True)  29.6 us
    dot_general x2, matrix products, local(): jnp.dot(gathered, up_weight, preferred_element_type=jnp.float32)  21.5 us
    dot_general x2, matrix products, local(): jnp.dot(hidden_all, down_weight, preferred_element_type=jnp.float32)  21.1 us
    ppermute x6, starting transfers between devices, local(): lax.ppermute(grown, 'neuron', [(d, d ^ reach) for d in range(ways)])  13.7 us
    psum x1, blocking collectives, local(): lax.psum((jnp.sum(residual_wide, axis=-1), jnp.sum(residual_wide * residu...  8.37 us
  transfers between devices with their start and end apart: 12, of which 11 were waited for; matrix products, arithmetic and copies ran while one was open for 8% of the time, Pallas kernels for 0%

profile of v1, /device:TPU:0, one launch (start us, length us, event | category | flops | bytes accessed | tf_op | source)
XLA Modules:
  0.0 390.1 jit_solution(14695434960364852051)
XLA Ops:
  6.5 1.2 convert_reduce_fusion.1
  7.7 1.2 fusion.26
  8.9 8.4 %all-reduce = (f32[32]{0:T(128)S(1)}, f32[32]{0:T(128)S(1)}, f32[32]{0:T(128)S(1)}, f32[32]{0:T(128)S(1)}) all-reduce(f32[32]{0:T(128)S(1)} %get-tuple-element.8, f32[32]{0:T(128)S(1)} %get-tuple-element.6, f32[32]{0:T(128)S(1)} %get-tuple-element.7, f32[32]{0:T(128)S(1)} %get-tuple-element.5), channel_id=1, replica_groups=mesh['batch'=4,'neuron'=8] {'batch'}, use_global_device_ids=true, to_apply=%region_10.11 | all-reduce | flops 128 | bytes 1024 | tf_op jit(solution)/shard_map/psum | solution.py:54
  17.3 1.3 fusion.25
  18.6 1.6 collective-permute-start.3
  20.2 4.2 %collective-permute-done.3 = bf16[32,3072]{1,0:T(8,128)(2,1)S(1)} collective-permute-done((bf16[32,3072]{1,0:T(8,128)(2,1)S(1)}, bf16[32,3072]{1,0:T(8,128)(2,1)S(1)}, u32[]{:S(2)}, u32[]{:S(2)}) %collective-permute-start.3) | collective-permute-done | bytes 196640 | tf_op jit(solution)/shard_map/ppermute | solution.py:62
  24.3 0.1 maximum_select_fusion.7
  24.4 1.6 collective-permute-start.4
  26.0 6.8 %collective-permute-done.4 = bf16[64,3072]{1,0:T(8,128)(2,1)S(1)} collective-permute-done((bf16[64,3072]{1,0:T(8,128)(2,1)S(1)}, bf16[64,3072]{1,0:T(8,128)(2,1)S(1)}, u32[]{:S(2)}, u32[]{:S(2)}) %collective-permute-start.4) | collective-permute-done | bytes 393248 | tf_op jit(solution)/shard_map/ppermute | solution.py:62
  32.8 0.2 maximum_select_fusion.5
  33.0 3.5 collective-permute-start.5
  36.4 30.5 %collective-permute-done.5 = bf16[128,3072]{1,0:T(8,128)(2,1)S(1)} collective-permute-done((bf16[128,3072]{1,0:T(8,128)(2,1)S(1)}, bf16[128,3072]{1,0:T(8,128)(2,1)S(1)}, u32[]{:S(2)}, u32[]{:S(2)}) %collective-permute-start.5) | collective-permute-done | bytes 786464 | tf_op jit(solution)/shard_map/ppermute | solution.py:62
  67.0 10.7 %fusion.6 = f32[256,3072]{1,0:T(8,128)} fusion(bf16[3072,3072]{1,0:T(8,128)(2,1)} %param.11, bf16[128,3072]{1,0:T(8,128)(2,1)S(1)} %collective-permute-done.5, bf16[128,3072]{1,0:T(8,128)(2,1)S(1)} %maximum_select_fusion.5, pred[]{:T(512)S(6)} %eq.26), kind=kOutput, calls=%fused_computation.8 | convolution fusion | flops 4838916096 | bytes 23592960 | tf_op jit(solution)/shard_map/dot_general | solution.py:69
  77.7 0.0 reduce-scatter.9.cloned.1.call-update
  77.7 0.0 reduce-scatter.5.cloned.1.call-start
  77.7 1.6 collective-permute-start
  79.4 4.1 %collective-permute-done = bf16[32,3072]{1,0:T(8,128)(2,1)S(1)} collective-permute-done((bf16[32,3072]{1,0:T(8,128)(2,1)S(1)}, bf16[32,3072]{1,0:T(8,128)(2,1)S(1)}, u32[]{:S(2)}, u32[]{:S(2)}) %collective-permute-start) | collective-permute-done | bytes 196640 | tf_op jit(solution)/shard_map/ppermute | solution.py:62
  83.5 0.1 maximum_select_fusion.6
  83.5 1.9 collective-permute-start.1
  85.5 8.4 %collective-permute-done.1 = bf16[64,3072]{1,0:T(8,128)(2,1)S(1)} collective-permute-done((bf16[64,3072]{1,0:T(8,128)(2,1)S(1)}, bf16[64,3072]{1,0:T(8,128)(2,1)S(1)}, u32[]{:S(2)}, u32[]{:S(2)}) %collective-permute-start.1) | collective-permute-done | bytes 393248 | tf_op jit(solution)/shard_map/ppermute | solution.py:62
  93.9 0.2 maximum_select_fusion.4
  94.1 3.5 collective-permute-start.2
  97.6 33.2 %collective-permute-done.2 = bf16[128,3072]{1,0:T(8,128)(2,1)S(1)} collective-permute-done((bf16[128,3072]{1,0:T(8,128)(2,1)S(1)}, bf16[128,3072]{1,0:T(8,128)(2,1)S(1)}, u32[]{:S(2)}, u32[]{:S(2)}) %collective-permute-start.2) | collective-permute-done | bytes 786464 | tf_op jit(solution)/shard_map/ppermute | solution.py:62
  130.7 10.8 %fusion = f32[256,3072]{1,0:T(8,128)} fusion(bf16[3072,3072]{1,0:T(8,128)(2,1)} %param.11, bf16[128,3072]{1,0:T(8,128)(2,1)S(1)} %collective-permute-done.2, bf16[128,3072]{1,0:T(8,128)(2,1)S(1)} %maximum_select_fusion.4, pred[]{:T(512)S(6)} %eq.26), kind=kOutput, calls=%fused_computation.1 | convolution fusion | flops 4838916096 | bytes 23592960 | tf_op jit(solution)/shard_map/dot_general | solution.py:69
  141.5 0.0 reduce-scatter.5.cloned.1.call-update
  141.5 0.0 all-gather.5.cloned.1.call-start
  141.6 0.6 copy-done.5
  142.2 0.2 compare_reduce_fusion.1
  142.4 0.2 fusion.38
  142.6 0.2 fusion.39
  142.8 40.4 %reduce-scatter.5.cloned.1.call-done = f32[64,3072]{1,0:T(8,128)} async-done(((f32[256,3072]{1,0:T(8,128)}), f32[64,3072]{1,0:T(8,128)}) %reduce-scatter.5.cloned.1.call-update) | async-done | bytes 786448 | tf_op jit(solution)/shard_map/reduce_scatter | solution.py:68
  183.2 0.3 mul.87
  183.4 0.3 mul.79
  183.7 0.6 copy-done.2
  184.3 1.3 fusion.15
  185.6 0.0 all-gather.3.cloned.1.call-start
  185.7 0.5 all-gather.3.cloned.1.call-update
  186.2 0.0 reduce-scatter.11.cloned.1.call-start
  186.3 19.2 %all-gather.5.cloned.1.call-done = bf16[256,3072]{1,0:T(8,128)(2,1)} async-done(((bf16[64,3072]{1,0:T(8,128)(2,1)}), bf16[256,3072]{1,0:T(8,128)(2,1)}) %all-gather.5.cloned.1.call-update) | async-done | bytes 1572880 | tf_op jit(solution)/shard_map/all_gather | solution.py:75
  205.4 10.5 %fusion.45 = f32[256,3072]{1,0:T(8,128)} fusion(bf16[256,3072]{1,0:T(8,128)(2,1)} %all-gather.5.cloned.1.call-done, bf16[3072,3072]{1,0:T(8,128)(2,1)} %param.13), kind=kOutput, calls=%fused_computation.72 | convolution fusion | flops 4831838208 | bytes 23592960 | tf_op jit(solution)/shard_map/dot_general | solution.py:77
  216.0 0.0 reduce-scatter.11.cloned.1.call-update
  216.0 0.0 reduce-scatter.7.cloned.1.call-start
  216.1 10.5 %all-gather.3.cloned.1.call-done = bf16[256,3072]{1,0:T(8,128)(2,1)} async-done(((bf16[64,3072]{1,0:T(8,128)(2,1)}), bf16[256,3072]{1,0:T(8,128)(2,1)}) %all-gather.3.cloned.1.call-update) | async-done | bytes 1572880 | tf_op jit(solution)/shard_map/all_gather | solution.py:75
  226.5 10.6 %fusion.44 = f32[256,3072]{1,0:T(8,128)} fusion(bf16[256,3072]{1,0:T(8,128)(2,1)} %all-gather.3.cloned.1.call-done, bf16[3072,3072]{1,0:T(8,128)(2,1)} %param.13), kind=kOutput, calls=%fused_computation.71 | convolution fusion | flops 4831838208 | bytes 23592960 | tf_op jit(solution)/shard_map/dot_general | solution.py:77
  237.2 67.0 %reduce-scatter.11.cloned.1.call-done = f32[32,3072]{1,0:T(8,128)} async-done(((f32[256,3072]{1,0:T(8,128)}), f32[32,3072]{1,0:T(8,128)}) %reduce-scatter.11.cloned.1.call-update) | async-done | bytes 393232 | tf_op jit(solution)/shard_map/reduce_scatter | solution.py:76
  304.1 77.2 %reduce-scatter.7.cloned.1.call-done = f32[32,3072]{1,0:T(8,128)} async-done(((f32[256,3072]{1,0:T(8,128)}), f32[32,3072]{1,0:T(8,128)}) %reduce-scatter.7.cloned.1.call-update) | async-done | bytes 393232 | tf_op jit(solution)/shard_map/reduce_scatter | solution.py:76
  381.3 1.2 fusion.37
  382.6 0.7 copy-done.6
  (20 shorter events, 0.1 us)
Async XLA Ops:
  6.5 136.2 %reduce-scatter.9.cloned.1.call-start = ((), (), s32[]{:S(2)}) async-start(), calls=%async_computation.7 | async-start | bytes 3932160 | tf_op jit(solution)/shard_map/reduce_scatter | solution.py:68
  18.6 5.7 %collective-permute-start.3 = (bf16[32,3072]{1,0:T(8,128)(2,1)S(1)}, bf16[32,3072]{1,0:T(8,128)(2,1)S(1)}, u32[]{:S(2)}, u32[]{:S(2)}) collective-permute-start(bf16[32,3072]{1,0:T(8,128)(2,1)S(1)} %get-tuple-element.16), channel_id=1, source_target_pairs={{0,1},{1,0},{2,3},{3,2},{4,5},{5,4},{6,7},{7,6},{8,9},{9,8},{10,11... | collective-permute-start | bytes 589832 | tf_op jit(solution)/shard_map/ppermute | solution.py:62
  24.4 8.4 %collective-permute-start.4 = (bf16[64,3072]{1,0:T(8,128)(2,1)S(1)}, bf16[64,3072]{1,0:T(8,128)(2,1)S(1)}, u32[]{:S(2)}, u32[]{:S(2)}) collective-permute-start(bf16[64,3072]{1,0:T(8,128)(2,1)S(1)} %maximum_select_fusion.7), channel_id=1, source_target_pairs={{0,2},{1,3},{2,0},{3,1},{4,6},{5,7},{6,4},{7,5},{8,10},{9,11},{10,... | collective-permute-start | bytes 1179656 | tf_op jit(solution)/shard_map/ppermute | solution.py:62
  33.0 34.0 %collective-permute-start.5 = (bf16[128,3072]{1,0:T(8,128)(2,1)S(1)}, bf16[128,3072]{1,0:T(8,128)(2,1)S(1)}, u32[]{:S(2)}, u32[]{:S(2)}) collective-permute-start(bf16[128,3072]{1,0:T(8,128)(2,1)S(1)} %maximum_select_fusion.5), channel_id=1, source_target_pairs={{0,4},{1,5},{2,6},{3,7},{4,0},{5,1},{6,2},{7,3},{8,12},{9,13},{10,... | collective-permute-start | bytes 2359304 | tf_op jit(solution)/shard_map/ppermute | solution.py:62
  77.7 105.5 %reduce-scatter.5.cloned.1.call-start = ((), (), s32[]{:S(2)}) async-start(), calls=%async_computation.4 | async-start | bytes 3932160 | tf_op jit(solution)/shard_map/reduce_scatter | solution.py:68
  77.7 5.7 %collective-permute-start = (bf16[32,3072]{1,0:T(8,128)(2,1)S(1)}, bf16[32,3072]{1,0:T(8,128)(2,1)S(1)}, u32[]{:S(2)}, u32[]{:S(2)}) collective-permute-start(bf16[32,3072]{1,0:T(8,128)(2,1)S(1)} %get-tuple-element.15), channel_id=1, source_target_pairs={{0,1},{1,0},{2,3},{3,2},{4,5},{5,4},{6,7},{7,6},{8,9},{9,8},{10,11... | collective-permute-start | bytes 589832 | tf_op jit(solution)/shard_map/ppermute | solution.py:62
  83.5 10.4 %collective-permute-start.1 = (bf16[64,3072]{1,0:T(8,128)(2,1)S(1)}, bf16[64,3072]{1,0:T(8,128)(2,1)S(1)}, u32[]{:S(2)}, u32[]{:S(2)}) collective-permute-start(bf16[64,3072]{1,0:T(8,128)(2,1)S(1)} %maximum_select_fusion.6), channel_id=1, source_target_pairs={{0,2},{1,3},{2,0},{3,1},{4,6},{5,7},{6,4},{7,5},{8,10},{9,11},{10,... | collective-permute-start | bytes 1179656 | tf_op jit(solution)/shard_map/ppermute | solution.py:62
  94.1 36.6 %collective-permute-start.2 = (bf16[128,3072]{1,0:T(8,128)(2,1)S(1)}, bf16[128,3072]{1,0:T(8,128)(2,1)S(1)}, u32[]{:S(2)}, u32[]{:S(2)}) collective-permute-start(bf16[128,3072]{1,0:T(8,128)(2,1)S(1)} %maximum_select_fusion.4), channel_id=1, source_target_pairs={{0,4},{1,5},{2,6},{3,7},{4,0},{5,1},{6,2},{7,3},{8,12},{9,13},{10,... | collective-permute-start | bytes 2359304 | tf_op jit(solution)/shard_map/ppermute | solution.py:62
  141.5 0.7 copy-start.5
  141.5 42.2 %copy-start.3 = (f32[3072]{0:T(1024)S(1)}, f32[3072]{0:T(1024)}, u32[]{:S(2)}) copy-start(f32[3072]{0:T(1024)} %param.12) | copy-start | bytes 36868
  141.5 63.9 %all-gather.5.cloned.1.call-start = ((), (), s32[]{:S(2)}) async-start(), calls=%async_computation.8 | async-start | bytes 1966080 | tf_op jit(solution)/shard_map/all_gather | solution.py:75
  142.8 40.9 %copy-start.1 = (f32[64,3072]{1,0:T(8,128)S(1)}, f32[64,3072]{1,0:T(8,128)}, u32[]{:S(2)}) copy-start(f32[64,3072]{1,0:T(8,128)} %reduce-scatter.9.cloned.1.call-done) | copy-start | bytes 2359300
  183.2 1.1 copy-start.2
  185.6 40.9 %all-gather.3.cloned.1.call-start = ((), (), s32[]{:S(2)}) async-start(), calls=%async_computation.5 | async-start | bytes 1966080 | tf_op jit(solution)/shard_map/all_gather | solution.py:75
  186.2 117.9 %reduce-scatter.11.cloned.1.call-start = ((), (), s32[]{:S(2)}) async-start(), calls=%async_computation.9 | async-start | bytes 3538944 | tf_op jit(solution)/shard_map/reduce_scatter | solution.py:76
  216.0 165.3 %reduce-scatter.7.cloned.1.call-start = ((), (), s32[]{:S(2)}) async-start(), calls=%async_computation.6 | async-start | bytes 3538944 | tf_op jit(solution)/shard_map/reduce_scatter | solution.py:76
  237.1 144.2 %copy-start = (bf16[2,32,3072]{2,1,0:T(8,128)(2,1)S(1)}, bf16[2,32,3072]{2,1,0:T(8,128)(2,1)}, u32[]{:S(2)}) copy-start(bf16[2,32,3072]{2,1,0:T(8,128)(2,1)} %param.8) | copy-start | bytes 1179652
  237.1 144.2 %copy-start.4 = (f32[3072]{0:T(1024)S(1)}, f32[3072]{0:T(1024)}, u32[]{:S(2)}) copy-start(f32[3072]{0:T(1024)} %param.14) | copy-start | bytes 36868
  382.5 0.7 copy-start.6
Sparse Core Ops, SparseCore 0:
  77.8 41.5 reduce-scatter.8
  141.6 41.4 reduce-scatter.4
  185.8 19.6 all-gather.4
  206.8 19.6 all-gather.2
  229.9 74.1 reduce-scatter.10
  307.6 73.6 reduce-scatter.6
